TPU v7x, 32 devices: a whole 2x2x4 slice. The times are simulated.
32 devices in a mesh: blk: 8 (over z, y), pix: 4 (over x, core).
Axes of the slice: x: 2, y: 2, z: 4, core: 2. Of those that a mesh axis runs over, the one named last changes fastest.
Arguments:
- images: bfloat16 [256, 16384], P('blk', 'pix'), may hold values from -14 to 14
- templates: bfloat16 [2304, 16384], P('blk', 'pix'), may hold values from -4 to 4
- routes: int32 [256, 4], P('blk'), may hold values from 0 to 7, all different within a row; in each aligned block of 32 rows (0 to 31, 32 to 63, ...) at most 24 rows name the same one
- image_weight: float32 [256], P('blk'), may hold values from 0.25 to 4
- template_weight: float32 [2304], P('blk'), may hold values from 0.25 to 4
Outputs:
- template_means: bfloat16 [2304, 16384], P('blk', 'pix')
- image_duals: float32 [256], P('blk')
Inputs may be any that keep to these rules, and one draw needn't show every extreme that they name: `routes`: each image names 4 different template blocks. Among the 32 images of one block, at most 24 name any one template block, and some template block is named by exactly 24 of them. Every template block is named by some image.
All inputs are finite; a program needn't handle non-finite values.
Results may differ from a plain program's by a relative error of at most 0.0046.
Values may be sent and summed in bfloat16 or wider, within the bound.
A program may use at most 64 MiB of HBM per device.

v0:
```python
import jax
import jax.numpy as jnp
from jax import lax
from jax.sharding import PartitionSpec as P

SWEEPS = 2


def on_device(images, templates, routes, image_weight, template_weight):
    blocks = lax.axis_size("blk")
    img_dev = images.shape[0]
    admits = routes.shape[1]
    capacity = max(2, (3 * img_dev * admits + 2 * blocks - 1) // (2 * blocks))
    target = routes.reshape(-1)
    target_hot = (target[:, None] == jnp.arange(blocks, dtype=jnp.int32)[None, :]).astype(jnp.int32)
    before = jnp.cumsum(target_hot, axis=0) - target_hot
    position = jnp.sum(before * target_hot, axis=1)
    slot_of = target * capacity + position
    wanted = jnp.arange(blocks * capacity, dtype=jnp.int32)
    matches = slot_of[None, :] == wanted[:, None]
    filled = jnp.any(matches, axis=1)
    owner_image = jnp.sum(
        jnp.where(matches, jnp.arange(target.shape[0], dtype=jnp.int32)[None, :] // admits, 0),
        axis=1,
    )
    outgoing = jnp.where(filled[:, None], images[owner_image], jnp.zeros((), images.dtype))
    outgoing = outgoing.reshape(blocks, capacity, images.shape[1])
    slot_flags = filled.astype(jnp.bfloat16).reshape(blocks, capacity)
    template_log = jnp.log(template_weight)
    arrived_piece = lax.all_to_all(outgoing, "blk", split_axis=0, concat_axis=0, tiled=True)
    marks_piece = lax.all_to_all(slot_flags, "blk", split_axis=0, concat_axis=0, tiled=True)
    partial_value = jnp.einsum(
        "bmp,tp->bmt", arrived_piece, templates, preferred_element_type=jnp.float32
    )
    summed = lax.psum(partial_value, "pix")
    usable = marks_piece > 0
    image_log = jnp.log(image_weight)
    slot_duals = jnp.zeros((blocks, capacity), jnp.float32)
    image_duals = jnp.zeros((img_dev,), jnp.float32)
    for sweep_index in range(SWEEPS):
        column_terms = jnp.where(usable[:, :, None], summed + slot_duals[:, :, None], -jnp.inf)
        column_peak = jnp.max(column_terms, axis=(0, 1))
        template_duals = (
            template_log
            - column_peak
            - jnp.log(jnp.sum(jnp.exp(column_terms - column_peak), axis=(0, 1)))
        )
        row_terms = summed + template_duals
        row_peak = jnp.max(row_terms, axis=2)
        row_total = jnp.sum(jnp.exp(row_terms - row_peak[:, :, None]), axis=2)
        levels = row_peak + jnp.log(row_total)
        back_levels = lax.all_to_all(levels, "blk", split_axis=0, concat_axis=0, tiled=True)
        level_routes = back_levels.reshape(-1)[slot_of].reshape(img_dev, admits)
        route_peak = jnp.max(level_routes, axis=1)
        image_duals = (
            image_log
            - route_peak
            - jnp.log(jnp.sum(jnp.exp(level_routes - route_peak[:, None]), axis=1))
        )
        duals_send = jnp.where(filled, image_duals[owner_image], 0.0).reshape(blocks, capacity)
        slot_duals = lax.all_to_all(duals_send, "blk", split_axis=0, concat_axis=0, tiled=True)
    column_terms = jnp.where(usable[:, :, None], summed + slot_duals[:, :, None], -jnp.inf)
    column_peak = jnp.max(column_terms, axis=(0, 1))
    column_exp = jnp.exp(column_terms - column_peak)
    plan_weights = (column_exp / jnp.sum(column_exp, axis=(0, 1))).astype(jnp.bfloat16)
    template_means = jnp.einsum(
        "bmt,bmp->tp", plan_weights, arrived_piece, preferred_element_type=jnp.float32
    ).astype(jnp.bfloat16)
    return (template_means, image_duals)


def solution(mesh):
    in_specs = (P("blk", "pix"), P("blk", "pix"), P("blk", None), P("blk"), P("blk"))
    out_specs = (P("blk", "pix"), P("blk"))
    return jax.shard_map(
        on_device, mesh=mesh, in_specs=in_specs, out_specs=out_specs, check_vma=False
    )
```

profile of v0, /device:TPU:0, one launch (start us, length us, event | category | flops | bytes accessed | tf_op | source)
XLA Modules:
  0.0 203.8 jit_solution(13468316568536961378)
XLA Ops:
  7.2 0.9 copy.17
  9.0 2.7 %gather_fusion = bf16[192,4096]{1,0:T(8,128)(2,1)} fusion(bf16[32,4096]{1,0:T(8,128)(2,1)S(1)} %copy-done.1, s32[1024]{0:T(1024)S(1)} %pad_clamp_fusion.1), kind=kCustom, calls=%fused_computation | custom fusion | bytes 3146496 | tf_op jit(solution)/shard_map/gather | solution.py:26
  11.7 2.7 %broadcast_select_fusion = bf16[8,24,4096]{2,1,0:T(8,128)(2,1)} fusion(bf16[8,24,4096]{2,1,0:T(8,128)(2,1)} %bitcast.88, pred[8,24]{1,0:T(8,128)(4,1)S(1)} %broadcast_in_dim.77), kind=kLoop, calls=%fused_computation.7 | loop fusion | flops 786432 | bytes 3145920 | tf_op jit(solution)/shard_map/jit(_where)/select_n | solution.py:26
  14.4 7.4 %all-to-all-start.1 = ((bf16[8,24,4096]{2,1,0:T(8,128)(2,1)}), bf16[8,24,4096]{2,1,0:T(8,128)(2,1)}, u32[]{:S(2)}, u32[]{:S(2)}) async-start(bf16[8,24,4096]{2,1,0:T(8,128)(2,1)} %broadcast_select_fusion), calls=%async_computation.1 | async-start | bytes 3145728 | tf_op jit(solution)/shard_map/all_to_all | solution.py:30
  22.8 36.2 %all-to-all-done.1 = bf16[8,24,4096]{2,1,0:T(8,128)(2,1)} async-done(((bf16[8,24,4096]{2,1,0:T(8,128)(2,1)}), bf16[8,24,4096]{2,1,0:T(8,128)(2,1)}, u32[]{:S(2)}, u32[]{:S(2)}) %all-to-all-start.1) | async-done | bytes 1572896 | tf_op jit(solution)/shard_map/all_to_all | solution.py:30
  59.0 3.6 %all-to-all-start = ((bf16[8,1,24]{2,1,0:T(2,128)(2,1)}), bf16[8,1,24]{2,1,0:T(2,128)(2,1)S(1)}, u32[]{:S(2)}, u32[]{:S(2)}) async-start(bf16[8,1,24]{2,1,0:T(2,128)(2,1)} %reshape.347), calls=%async_computation | async-start | bytes 8192 | tf_op jit(solution)/shard_map/all_to_all | solution.py:31
  62.7 3.3 %fusion.1 = f32[8,24,288]{2,1,0:T(8,128)} fusion(bf16[8,24,4096]{2,1,0:T(8,128)(2,1)} %all-to-all-done.1, bf16[288,4096]{1,0:T(8,128)(2,1)S(1)} %copy-done), kind=kOutput, calls=%fused_computation.5 | convolution fusion | flops 452984832 | bytes 4153344 | tf_op jit(solution)/shard_map/bmp,tp->bmt/dot_general | solution.py:32
  66.0 3.1 %all-to-all-done = bf16[8,1,24]{2,1,0:T(2,128)(2,1)S(1)} async-done(((bf16[8,1,24]{2,1,0:T(2,128)(2,1)}), bf16[8,1,24]{2,1,0:T(2,128)(2,1)S(1)}, u32[]{:S(2)}, u32[]{:S(2)}) %all-to-all-start) | async-done | bytes 416 | tf_op jit(solution)/shard_map/all_to_all | solution.py:31
  69.1 31.1 %all-reduce.2.cloned.1.call-done = f32[8,24,288]{2,1,0:T(8,128)} async-done(((f32[8,24,288]{2,1,0:T(8,128)}), f32[8,24,288]{2,1,0:T(8,128)}) %all-reduce.2.cloned.1.call-update) | async-done | bytes 221200 | tf_op jit(solution)/shard_map/psum | solution.py:35
  100.2 1.1 select_reduce_fusion
  101.3 1.1 exponential_reduce_fusion.3
  102.5 1.1 add_reduce_fusion.1
  103.5 1.2 exponential_reduce_fusion.2
  105.3 5.5 %all-to-all-start.2 = ((f32[8,1,24]{2,1,0:T(1,128)}), f32[8,1,24]{2,1,0:T(1,128)S(1)}, u32[]{:S(2)}, u32[]{:S(2)}) async-start(f32[8,1,24]{2,1,0:T(1,128)} %bitcast.5), calls=%async_computation.2 | async-start | bytes 8192 | tf_op jit(solution)/shard_map/all_to_all | solution.py:52
  110.8 6.4 %all-to-all-done.2 = f32[8,1,24]{2,1,0:T(1,128)S(1)} async-done(((f32[8,1,24]{2,1,0:T(1,128)}), f32[8,1,24]{2,1,0:T(1,128)S(1)}, u32[]{:S(2)}, u32[]{:S(2)}) %all-to-all-start.2) | async-done | bytes 800 | tf_op jit(solution)/shard_map/all_to_all | solution.py:52
  118.5 1.3 gather_fusion.1
  121.6 19.9 %select_select_fusion.1 = f32[192]{0:T(256)S(1)} fusion(pred[192]{0:T(512)(128)(4,1)S(1)} %fusion.11, f32[]{:T(128)} %bitcast.8, f32[]{:T(128)} %bitcast.9, f32[]{:T(128)} %bitcast.10, f32[]{:T(128)} %bitcast.11, f32[]{:T(128)} %bitcast.12, f32[]{:T(128)} %bitcast.13, f32[]{:T(128)} %bitcast.14, f32[]{:T(128)} %bitcast.15, f32[]{:T(128)} %bitcast.16, ...), kind=kLoop, calls=%fused_computation.46 | loop fusion | flops 12096 | bytes 1856 | tf_op jit(solution)/shard_map/jit(_where)/select_n | solution.py:60
  141.6 8.8 %all_to_all.35 = f32[8,1,24]{2,1,0:T(1,128)S(1)} all-to-all(f32[8,1,24]{2,1,0:T(1,128)S(1)} %select_n.88), channel_id=1, replica_groups=mesh['blk'=8,'pix'=4] {'blk'}, dimensions={0} | all-to-all | bytes 1536 | tf_op jit(solution)/shard_map/all_to_all | solution.py:61
  151.1 8.9 %all_to_all.36 = f32[8,1,24]{2,1,0:T(1,128)S(1)} all-to-all(f32[8,1,24]{2,1,0:T(1,128)S(1)} %bitcast.97), channel_id=1, replica_groups=mesh['blk'=8,'pix'=4] {'blk'}, dimensions={0} | all-to-all | bytes 1536 | tf_op jit(solution)/shard_map/all_to_all | solution.py:52
  160.7 1.3 gather_fusion.2
  163.1 0.7 fusion.15
  163.8 20.1 %select_select_fusion = f32[192]{0:T(256)S(1)} fusion(pred[192]{0:T(512)(128)(4,1)S(1)} %fusion.11, f32[]{:T(128)} %bitcast.42, f32[]{:T(128)} %bitcast.43, f32[]{:T(128)} %bitcast.44, f32[]{:T(128)} %bitcast.45, f32[]{:T(128)} %bitcast.46, f32[]{:T(128)} %bitcast.47, f32[]{:T(128)} %bitcast.48, f32[]{:T(128)} %bitcast.49, f32[]{:T(128)} %bitcast.50, ...), kind=kLoop, calls=%fused_computation.45 | loop fusion | flops 12096 | bytes 1856 | tf_op jit(solution)/shard_map/jit(_where)/select_n | solution.py:60
  184.0 8.8 %all_to_all.37 = f32[8,1,24]{2,1,0:T(1,128)S(1)} all-to-all(f32[8,1,24]{2,1,0:T(1,128)S(1)} %select_n.91), channel_id=1, replica_groups=mesh['blk'=8,'pix'=4] {'blk'}, dimensions={0} | all-to-all | bytes 1536 | tf_op jit(solution)/shard_map/all_to_all | solution.py:61
  193.2 3.7 %fusion = bf16[288,4096]{1,0:T(8,128)(2,1)} fusion(bf16[8,24,4096]{2,1,0:T(8,128)(2,1)} %all-to-all-done.1, f32[8,24,288]{2,1,0:T(8,128)S(1)} %copy-done.2, f32[288]{0:T(512)S(1)} %fusion.5, f32[288]{0:T(512)S(1)} %fusion.4, f32[8,24]{1,0:T(8,128)S(1)} %bitcast.91, pred[8,24]{1,0:T(8,128)(4,1)S(1)} %compare_bitcast_fusion), kind=kOutput, calls=%fused_computation.4 | convolution fusion | flops 454440960 | bytes 4156608 | tf_op jit(solution)/shard_map/bmt,bmp->tp/dot_general | solution.py:66
  (62 shorter events, 8.5 us)
Async XLA Ops:
  7.2 55.5 %copy-start = (bf16[288,4096]{1,0:T(8,128)(2,1)S(1)}, bf16[288,4096]{1,0:T(8,128)(2,1)}, u32[]{:S(2)}) copy-start(bf16[288,4096]{1,0:T(8,128)(2,1)} %param.6) | copy-start | bytes 7077892
  7.2 1.8 copy-start.1
  14.4 7.5 %copy-start.4 = (s32[32,4]{0,1:T(4,128)S(1)}, s32[32,4]{0,1:T(4,128)}, u32[]{:S(2)}) copy-start(s32[32,4]{0,1:T(4,128)} %param.7) | copy-start | bytes 1540
  14.4 44.5 %all-to-all-start.1 = ((bf16[8,24,4096]{2,1,0:T(8,128)(2,1)}), bf16[8,24,4096]{2,1,0:T(8,128)(2,1)}, u32[]{:S(2)}, u32[]{:S(2)}) async-start(bf16[8,24,4096]{2,1,0:T(8,128)(2,1)} %broadcast_select_fusion), calls=%async_computation.1 | async-start | bytes 3145728 | tf_op jit(solution)/shard_map/all_to_all | solution.py:30
  59.0 10.1 %all-to-all-start = ((bf16[8,1,24]{2,1,0:T(2,128)(2,1)}), bf16[8,1,24]{2,1,0:T(2,128)(2,1)S(1)}, u32[]{:S(2)}, u32[]{:S(2)}) async-start(bf16[8,1,24]{2,1,0:T(2,128)(2,1)} %reshape.347), calls=%async_computation | async-start | bytes 8192 | tf_op jit(solution)/shard_map/all_to_all | solution.py:31
  62.6 39.8 %copy-start.5 = (f32[288]{0:T(512)S(1)}, f32[288]{0:T(512)}, u32[]{:S(2)}) copy-start(f32[288]{0:T(512)} %param.9) | copy-start | bytes 3460
  62.6 37.6 %all-reduce.2.cloned.1.call-start = ((), (), s32[]{:S(2)}) async-start(), calls=%async_computation.6 | async-start | bytes 589824 | tf_op jit(solution)/shard_map/psum | solution.py:35
  66.0 54.2 %copy-start.6 = (f32[32]{0:T(128)S(1)}, f32[32]{0:T(128)}, u32[]{:S(2)}) copy-start(f32[32]{0:T(128)} %param.8) | copy-start | bytes 388
  100.2 50.3 %copy-start.2 = (f32[8,24,288]{2,1,0:T(8,128)S(1)}, f32[8,24,288]{2,1,0:T(8,128)}, u32[]{:S(2)}) copy-start(f32[8,24,288]{2,1,0:T(8,128)} %all-reduce.2.cloned.1.call-done) | copy-start | bytes 663556
  105.3 11.9 %all-to-all-start.2 = ((f32[8,1,24]{2,1,0:T(1,128)}), f32[8,1,24]{2,1,0:T(1,128)S(1)}, u32[]{:S(2)}, u32[]{:S(2)}) async-start(f32[8,1,24]{2,1,0:T(1,128)} %bitcast.5), calls=%async_computation.2 | async-start | bytes 8192 | tf_op jit(solution)/shard_map/all_to_all | solution.py:52
  162.4 34.5 %copy-start.3 = (f32[32]{0:T(128)}, f32[32]{0:T(128)S(1)}, u32[]{:S(2)}) copy-start(f32[32]{0:T(128)S(1)} %log_subtract_fusion.2) | copy-start | bytes 388
Sparse Core Ops, SparseCore 0:
  66.3 33.7 all-reduce.1
where the time goes:
time: 205 us; the launch traced here: 204 us
  waiting for transfers between devices  76.8 us (37%)
  other arithmetic  51.3 us (25%)
  blocking collectives  26.6 us (13%)
  starting transfers between devices  16.6 us (8%)
  between operations  14.3 us (7%)
  local copies, waits for them, and re-layouts  11.1 us (5%)
  matrix products  7.05 us (3%)
    select_n x2, other arithmetic, on_device(): jnp.where(filled, image_duals[owner_image], 0.0).reshape(blocks, capacity)  40 us
    all_to_all x1, waiting for transfers between devices, on_device(): lax.all_to_all(outgoing, 'blk', split_axis=0, concat_axis=0, tiled=True)  36.2 us
    psum x1, waiting for transfers between devices, on_device(): summed = lax.psum(partial_value, 'pix')  31.1 us
    all_to_all x2, blocking collectives, on_device(): lax.all_to_all(duals_send, 'blk', split_axis=0, concat_axis=0, tiled=True)  17.7 us
    all_to_all x1, blocking collectives, on_device(): lax.all_to_all(levels, 'blk', split_axis=0, concat_axis=0, tiled=True)  8.86 us
    all_to_all x1, starting transfers between devices, on_device(): lax.all_to_all(outgoing, 'blk', split_axis=0, concat_axis=0, tiled=True)  7.44 us
    all_to_all x1, waiting for transfers between devices, on_device(): lax.all_to_all(levels, 'blk', split_axis=0, concat_axis=0, tiled=True)  6.41 us
    all_to_all x1, starting transfers between devices, on_device(): lax.all_to_all(levels, 'blk', split_axis=0, concat_axis=0, tiled=True)  5.52 us
  transfers between devices with their start and end apart: 4, of which 4 were waited for; matrix products, arithmetic and copies ran while one was open for 2% of the time, Pallas kernels for 0%

commit v1 on v0

--- a/solution.py
+++ b/solution.py
@@ -1,12 +1,21 @@
+import functools
 import jax
 import jax.numpy as jnp
 from jax import lax
+from jax.experimental import pallas as pl
+from jax.experimental.pallas import tpu as pltpu
 from jax.sharding import PartitionSpec as P
 
 SWEEPS = 2
-
-
-def on_device(images, templates, routes, image_weight, template_weight):
+LINES = 2
+CHUNKS = 8
+LAG = 2
+NEG = -1e30
+MESH = pl.DeviceIdType.MESH
+UP, DOWN, ACROSS = 0, 1, 2
+
+
+def routed(images, templates, routes, image_weight, template_weight):
     blocks = lax.axis_size("blk")
     img_dev = images.shape[0]
     admits = routes.shape[1]
@@ -69,6 +78,297 @@
     return (template_means, image_duals)
 
 
+def gather_and_plan(dims, img_hbm, tpl_hbm, info_ref, tlog_ref, gath_hbm, plan_ref, dual_ref,
+                    buf, infos, tpl, acc, parts, lse_out, lse_in,
+                    send_sem, recv_sem, info_send, info_recv, local_sem,
+                    part_send, part_recv, lse_send, lse_recv, plan_send, plan_recv):
+    blocks, pixes, admits, tpl_dev, share = dims
+    depth = blocks // LINES
+    rows, pixels = img_hbm.shape
+    width = pixels // CHUNKS
+    b, p = lax.axis_index("blk"), lax.axis_index("pix")
+    z, y = b // LINES, b % LINES
+    other = 1 - y
+    has_up, has_down = z < depth - 1, z > 0
+    target = {UP: b + LINES, DOWN: b - LINES, ACROSS: z * LINES + other}
+    allowed = {UP: has_up, DOWN: has_down}
+
+    tpl_copy = pltpu.make_async_copy(tpl_hbm, tpl, local_sem.at[0])
+    own_copy = pltpu.make_async_copy(img_hbm, buf.at[b], local_sem.at[1])
+    info_copy = pltpu.make_async_copy(info_ref, infos.at[b], local_sem.at[2])
+    tpl_copy.start()
+    own_copy.start()
+    info_copy.start()
+
+    barrier = pltpu.get_barrier_semaphore()
+    for way in (UP, DOWN):
+        @pl.when(allowed[way])
+        def _():
+            pl.semaphore_signal(barrier, inc=1, device_id={"blk": target[way]}, device_id_type=MESH)
+    pl.semaphore_signal(barrier, inc=1, device_id={"blk": target[ACROSS]}, device_id_type=MESH)
+    for j in range(1, pixes):
+        pl.semaphore_signal(barrier, inc=1, device_id={"pix": lax.rem(p + j, pixes)}, device_id_type=MESH)
+    near = jnp.where(has_up, 1, 0) + jnp.where(has_down, 1, 0) + pixes
+    pl.semaphore_wait(barrier, near)
+
+    def cols(c):
+        return pl.ds(c * width, width)
+
+    def piece(way, k, c, own=False):
+        return pltpu.make_async_remote_copy(
+            src_ref=img_hbm.at[:, cols(c)] if own else buf.at[k, :, cols(c)],
+            dst_ref=buf.at[k, :, cols(c)],
+            send_sem=send_sem.at[way, k], recv_sem=recv_sem.at[k, c],
+            device_id={"blk": target[way]}, device_id_type=MESH)
+
+    def info_piece(way, k, own=False):
+        return pltpu.make_async_remote_copy(
+            src_ref=info_ref if own else infos.at[k], dst_ref=infos.at[k],
+            send_sem=info_send.at[way, k], recv_sem=info_recv.at[k],
+            device_id={"blk": target[way]}, device_id_type=MESH)
+
+    def arrived(k, c):
+        pltpu.make_async_copy(buf.at[k, :, cols(c)], buf.at[k, :, cols(c)], recv_sem.at[k, c]).wait()
+
+    def info_arrived(k):
+        pltpu.make_async_copy(infos.at[k], infos.at[k], info_recv.at[k]).wait()
+
+    def along(way, start):
+        @pl.when(allowed[way])
+        def _():
+            start()
+
+    for c in range(CHUNKS):
+        piece(ACROSS, b, c, True).start()
+        for way in (UP, DOWN):
+            along(way, lambda: piece(way, b, c, True).start())
+    info_piece(ACROSS, b, True).start()
+    for way in (UP, DOWN):
+        along(way, lambda: info_piece(way, b, True).start())
+    mate = z * LINES + other
+    arrived(mate, 0)
+    for way in (UP, DOWN):
+        along(way, lambda: piece(way, mate, 0).start())
+
+    def sides(d):
+        return ((UP, z - d, z >= d), (DOWN, z + d, z + d < depth))
+
+    def pass_on(d, c):
+        for way, from_z, there in sides(d):
+            k = from_z * LINES + y
+
+            @pl.when(there)
+            def _():
+                arrived(k, c)
+                if c:
+                    piece(ACROSS, k, c).start()
+                along(way, lambda: piece(way, k, c).start())
+
+    def pass_rest(d):
+        for way, from_z, there in sides(d):
+            k, k2 = from_z * LINES + y, from_z * LINES + other
+
+            @pl.when(there)
+            def _():
+                arrived(k2, 0)
+                along(way, lambda: piece(way, k2, 0).start())
+                info_arrived(k)
+                info_piece(ACROSS, k).start()
+                along(way, lambda: info_piece(way, k).start())
+
+    def crossed(c):
+        if c:
+            arrived(mate, c)
+            for d in range(1, depth):
+                for way, from_z, there in sides(d):
+                    @pl.when(there)
+                    def _():
+                        arrived(from_z * LINES + other, c)
+
+    def product(c):
+        images = buf[:, :, c * width:(c + 1) * width].reshape(blocks * rows, width)
+        term = lax.dot_general(tpl[:, c * width:(c + 1) * width], images, (((1,), (1,)), ((), ())),
+                               preferred_element_type=jnp.float32)
+        if c == 1:
+            acc[0:tpl_dev, :] = term
+        else:
+            acc[0:tpl_dev, :] += term
+
+    for d in range(1, depth - 1):
+        for c in range(CHUNKS):
+            pass_on(d, c)
+        pass_rest(d)
+    own_copy.wait()
+    tpl_copy.wait()
+    if share * pixes > tpl_dev:
+        acc[tpl_dev:, :] = jnp.zeros((share * pixes - tpl_dev, blocks * rows), jnp.float32)
+    for c in range(CHUNKS + LAG):
+        if c < CHUNKS:
+            pass_on(depth - 1, c)
+        if c == CHUNKS - 1:
+            pass_rest(depth - 1)
+        if c == CHUNKS + LAG - 1:
+            product(0)
+        if c > LAG:
+            crossed(c - LAG)
+            product(c - LAG)
+
+    def my_part(j):
+        return pltpu.make_async_remote_copy(
+            src_ref=acc.at[pl.ds(lax.rem(p + j, pixes) * share, share), :], dst_ref=parts.at[j - 1],
+            send_sem=part_send.at[j - 1], recv_sem=part_recv.at[j - 1],
+            device_id={"pix": lax.rem(p + j, pixes)}, device_id_type=MESH)
+
+    for j in range(1, pixes):
+        my_part(j).start()
+    back = pltpu.make_async_copy(buf, gath_hbm, local_sem.at[3])
+    back.start()
+
+    info_copy.wait()
+    info_arrived(mate)
+    for d in range(1, depth):
+        for way, from_z, there in sides(d):
+            @pl.when(there)
+            def _():
+                info_arrived(from_z * LINES + other)
+    info = jnp.sum(infos[...], axis=0)
+    code = (b + 1).astype(jnp.float32)
+    admitted = jnp.max(jnp.where(info[0:admits, :] == code, 1.0, 0.0), axis=0, keepdims=True)
+    image_log = info[admits:admits + 1, :]
+    first = p * share
+    template_log = tlog_ref[pl.ds(pl.multiple_of(first, 16), share), :]
+    valid = first + lax.broadcasted_iota(jnp.int32, (share, 1), 0) < tpl_dev
+    scores = acc[pl.ds(pl.multiple_of(first, 16), share), :]
+    for j in range(1, pixes):
+        my_part(j).wait_recv()
+        scores = scores + parts[j - 1]
+    scores = jnp.where(admitted > 0, scores, NEG)
+
+    me = b * pixes + p
+    devices = blocks * pixes
+    duals = jnp.zeros((1, blocks * rows), jnp.float32)
+    for sweep in range(SWEEPS):
+        terms = scores + duals
+        peak = jnp.max(terms, axis=1, keepdims=True)
+        level = template_log - peak - jnp.log(jnp.sum(jnp.exp(terms - peak), axis=1, keepdims=True))
+        level = jnp.where(valid, level, NEG)
+        terms = scores + level
+        peak = jnp.max(terms, axis=0, keepdims=True)
+        lse = peak + jnp.log(jnp.sum(jnp.exp(terms - peak), axis=0, keepdims=True))
+        lse_out[sweep] = lse
+
+        def post(j, carry):
+            to = lax.rem(me + j, devices)
+            pltpu.make_async_remote_copy(
+                src_ref=lse_out.at[sweep], dst_ref=lse_in.at[sweep, me],
+                send_sem=lse_send.at[sweep], recv_sem=lse_recv.at[sweep],
+                device_id={"blk": to // pixes, "pix": lax.rem(to, pixes)}, device_id_type=MESH).start()
+            return carry
+
+        lax.fori_loop(1, devices, post, 0)
+        lse_in[sweep, me] = lse
+        span = lse_in.at[sweep, pl.ds(0, devices - 1)]
+        pltpu.make_async_copy(span, span, lse_recv.at[sweep]).wait()
+        every = lse_in[sweep]
+        peak = jnp.max(every, axis=0)
+        duals = image_log - peak - jnp.log(jnp.sum(jnp.exp(every - peak), axis=0))
+    dual_ref[...] = duals
+    terms = scores + duals
+    weight = jnp.exp(terms - jnp.max(terms, axis=1, keepdims=True))
+    mine = pl.ds(pl.multiple_of(first, 16), share)
+    plan_ref[mine, :] = (weight / jnp.sum(weight, axis=1, keepdims=True)).astype(jnp.bfloat16)
+
+    def my_plan(j):
+        return pltpu.make_async_remote_copy(
+            src_ref=plan_ref.at[mine, :], dst_ref=plan_ref.at[mine, :],
+            send_sem=plan_send.at[j - 1], recv_sem=plan_recv.at[j - 1],
+            device_id={"pix": lax.rem(p + j, pixes)}, device_id_type=MESH)
+
+    for j in range(1, pixes):
+        my_plan(j).start()
+
+    full = buf.at[b]
+    rest = buf.at[b, :, pl.ds(width, pixels - width)]
+    one = buf.at[b, :, pl.ds(0, width)]
+
+    def left(ref, sem):
+        pltpu.make_async_copy(ref, ref, sem).wait()
+
+    left(full, send_sem.at[ACROSS, b])
+    left(infos.at[b], info_send.at[ACROSS, b])
+    for way in (UP, DOWN):
+        along(way, lambda: (left(full, send_sem.at[way, b]), left(one, send_sem.at[way, mate]),
+                            left(infos.at[b], info_send.at[way, b])) and None)
+    for d in range(1, depth):
+        for way, from_z, there in sides(d):
+            k, k2 = from_z * LINES + y, from_z * LINES + other
+
+            @pl.when(there)
+            def _():
+                left(rest, send_sem.at[ACROSS, k])
+                left(infos.at[b], info_send.at[ACROSS, k])
+                along(way, lambda: (left(full, send_sem.at[way, k]), left(one, send_sem.at[way, k2]),
+                                    left(infos.at[b], info_send.at[way, k])) and None)
+    for j in range(1, pixes):
+        my_part(j).wait_send()
+    for sweep in range(SWEEPS):
+        span = lse_in.at[sweep, pl.ds(0, devices - 1)]
+        left(span, lse_send.at[sweep])
+    back.wait()
+    for j in range(1, pixes):
+        my_plan(j).wait_send()
+        my_plan(j).wait_recv()
+
+
+def gathered(images, templates, routes, image_weight, template_weight):
+    blocks, pixes = lax.axis_size("blk"), lax.axis_size("pix")
+    rows, pixels = images.shape
+    tpl_dev, admits = templates.shape[0], routes.shape[1]
+    share = -(-tpl_dev // (16 * pixes)) * 16
+    b = lax.axis_index("blk")
+    info = jnp.concatenate([routes.T.astype(jnp.float32) + 1.0, jnp.log(image_weight)[None, :]], axis=0)
+    info = jnp.pad(info, ((0, -(admits + 1) % 8), (0, 0)))
+    deep = info.shape[0]
+    spot = jnp.arange(blocks * rows, dtype=jnp.int32)[None, :] // rows == b
+    info = jnp.where(spot, jnp.tile(info, (1, blocks)), 0.0)
+    tlog = jnp.pad(jnp.log(template_weight), (0, share * pixes - tpl_dev))[:, None]
+    dims = (blocks, pixes, admits, tpl_dev, share)
+    any_spec, vmem = pl.BlockSpec(memory_space=pl.ANY), pl.BlockSpec(memory_space=pltpu.VMEM)
+    dma = pltpu.SemaphoreType.DMA
+    devices = blocks * pixes
+    gath, plan, duals = pl.pallas_call(
+        functools.partial(gather_and_plan, dims),
+        out_shape=(jax.ShapeDtypeStruct((blocks, rows, pixels), images.dtype),
+                   jax.ShapeDtypeStruct((share * pixes, blocks * rows), jnp.bfloat16),
+                   jax.ShapeDtypeStruct((1, blocks * rows), jnp.float32)),
+        in_specs=[any_spec, any_spec, vmem, vmem],
+        out_specs=(any_spec, vmem, vmem),
+        scratch_shapes=[
+            pltpu.VMEM((blocks, rows, pixels), images.dtype),
+            pltpu.VMEM((blocks, deep, blocks * rows), jnp.float32),
+            pltpu.VMEM((tpl_dev, pixels), templates.dtype),
+            pltpu.VMEM((share * pixes, blocks * rows), jnp.float32),
+            pltpu.VMEM((pixes - 1, share, blocks * rows), jnp.float32),
+            pltpu.VMEM((SWEEPS, 1, blocks * rows), jnp.float32),
+            pltpu.VMEM((SWEEPS, devices, 1, blocks * rows), jnp.float32),
+            dma((3, blocks)), dma((blocks, CHUNKS)), dma((3, blocks)), dma((blocks,)), dma((4,)),
+            dma((pixes - 1,)), dma((pixes - 1,)), dma((SWEEPS,)), dma((SWEEPS,)),
+            dma((pixes - 1,)), dma((pixes - 1,)),
+        ],
+        compiler_params=pltpu.CompilerParams(collective_id=0, has_side_effects=True),
+    )(images, templates, info, tlog)
+    means = jnp.einsum("ti,ip->tp", plan[:tpl_dev], gath.reshape(blocks * rows, pixels),
+                       preferred_element_type=jnp.float32).astype(jnp.bfloat16)
+    return means, lax.dynamic_slice(duals.reshape(-1), (b * rows,), (rows,))
+
+
+def on_device(images, templates, routes, image_weight, template_weight):
+    blocks = lax.axis_size("blk")
+    if blocks * images.shape[0] <= templates.shape[0] and blocks % LINES == 0:
+        return gathered(images, templates, routes, image_weight, template_weight)
+    return routed(images, templates, routes, image_weight, template_weight)
+
+
 def solution(mesh):
     in_specs = (P("blk", "pix"), P("blk", "pix"), P("blk", None), P("blk"), P("blk"))
     out_specs = (P("blk", "pix"), P("blk"))

time: 205 us -> 61 us (0.30)
  waiting for transfers between devices: 76.8 us -> 0 us
  Pallas kernels: 0 us -> 51.4 us
  other arithmetic: 51.3 us -> 1.32 us
  blocking collectives: 26.6 us -> 0 us
  starting transfers between devices: 16.6 us -> 0 us
  between operations: 14.3 us -> 0.65 us
  local copies, waits for them, and re-layouts: 11.1 us -> 3.46 us
  matrix products: 7.05 us -> 3.87 us
    pallas_call x0 -> x1, Pallas kernels: none -> 51.4 us  [gathered(): pl.pallas_call(functools.partial(gather_and_plan, dims), out_shape=(jax.S...]
    all_to_all x3 -> x0, waiting for transfers between devices: 45.7 us -> none  [the longest x1 36.2 us: on_device(): lax.all_to_all(outgoing, 'blk', split_axis=0, concat_axis=0, tiled=True)]
    select_n x6 -> x1, other arithmetic: 42.7 us -> 0.61 us  [gathered(): info = jnp.where(spot, jnp.tile(info, (1, blocks)), 0.0)]
    psum x1 -> x0, waiting for transfers between devices: 31.1 us -> none  [on_device(): summed = lax.psum(partial_value, 'pix')]
    all_to_all x3 -> x0, blocking collectives: 26.6 us -> none  [the longest x2 17.7 us: on_device(): lax.all_to_all(duals_send, 'blk', split_axis=0, concat_axis=0, tiled=True)]
    all_to_all x3 -> x0, starting transfers between devices: 16.6 us -> none  [the longest x1 7.44 us: on_device(): lax.all_to_all(outgoing, 'blk', split_axis=0, concat_axis=0, tiled=True)]
    gather x7 -> x0, local copies, waits for them, and re-layouts: 8.05 us -> none  [the longest x4 2.85 us: on_device(): image_duals[owner_image]]
    reduce_sum x9 -> x0, other arithmetic: 3.42 us -> none  [the longest x2 1.34 us: on_device(): row_total = jnp.sum(jnp.exp(row_terms - row_peak[:, :, None]), axis=2)]
  transfers between devices with their start and end apart: 4 -> 0, of which waited for: 4 -> 0; matrix products, arithmetic and copies ran while one was open for 2% -> 0% of each run, Pallas kernels for 0% -> 0%
where the time goes in v1:
time: 61 us; the launch traced here: 60.7 us
  Pallas kernels  51.4 us (84%)
  matrix products  3.87 us (6%)
  local copies, waits for them, and re-layouts  3.46 us (6%)
  other arithmetic  1.32 us (2%)
  between operations  0.65 us (1%)
    pallas_call x1, Pallas kernels, gathered(): pl.pallas_call(functools.partial(gather_and_plan, dims), out_shape=(jax.S...  51.4 us
    dot_general x1, matrix products, gathered(): jnp.einsum('ti,ip->tp', plan[:tpl_dev], gath.reshape(blocks * rows, pixel...  3.87 us
    dynamic_slice x1, local copies, waits for them, and re-layouts, gathered(): return (means, lax.dynamic_slice(duals.reshape(-1), (b * rows,), (rows,)))  1.25 us

profile of v1, /device:TPU:0, one launch (start us, length us, event | category | flops | bytes accessed | tf_op | source)
XLA Modules:
  0.0 60.7 jit_solution(9747504014547571730)
XLA Ops:
  0.6 0.7 %log_bitcast_fusion = f32[1,32]{1,0:T(1,128)S(1)} fusion(f32[32]{0:T(128)} %param.8), kind=kLoop, calls=%fused_computation.12 | loop fusion | bytes 256 | tf_op jit(solution)/shard_map/broadcast_in_dim | solution.py:329
  1.3 0.7 %add_bitcast_fusion = f32[4,32]{1,0:T(4,128)S(1)} fusion(s32[32,4]{0,1:T(4,128)} %param.7), kind=kLoop, calls=%fused_computation.5 | loop fusion | flops 256 | bytes 1024 | tf_op jit(solution)/shard_map/add | solution.py:329
  2.0 0.7 %log.7 = f32[288]{0:T(512)S(1)} log(f32[288]{0:T(512)} %param.9) | non-fusion elementwise | bytes 2304 | tf_op jit(solution)/shard_map/log | solution.py:334
  2.7 0.1 tile.10
  2.8 0.6 %broadcast_select_fusion.info_ref = f32[8,256]{1,0:T(8,128)} fusion(f32[8,256]{1,0:T(8,128)S(1)} %tile.10, pred[256]{0:T(512)(128)(4,1)S(1)} %fusion.1), kind=kLoop, calls=%fused_computation.4 | loop fusion | flops 2048 | bytes 16640 | tf_op jit(solution)/shard_map/jit(_where)/select_n | solution.py:333
  3.4 0.8 %broadcast_in_dim.23.tlog_ref = f32[320,1]{1,0:T(8,128)} reshape(f32[320]{0:T(512)S(1)} %pad.9) | data formatting | bytes 2560 | tf_op jit(solution)/shard_map/broadcast_in_dim | solution.py:334
  4.2 51.4 %shard_map.68 = (bf16[8,32,4096]{2,1,0:T(8,128)(2,1)}, bf16[320,256]{1,0:T(8,128)(2,1)}, f32[1,256]{1,0:T(1,128)}) custom-call(bf16[32,4096]{1,0:T(8,128)(2,1)} %img_hbm.1, bf16[288,4096]{1,0:T(8,128)(2,1)} %tpl_hbm.1, f32[8,256]{1,0:T(8,128)} %broadcast_select_fusion.info_ref, f32[320,1]{1,0:T(8,128)} %broadcast_in_dim.23.tlog_ref), custom_call_target="tpu_custom_call" | custom-call | tf_op jit(solution)/shard_map/pallas_call | solution.py:339
  55.6 1.3 %dynamic-slice_bitcast_fusion = f32[32]{0:T(128)} fusion(f32[1,256]{1,0:T(1,128)} %get-tuple-element.7, s32[]{:T(128)S(6)} %select_n.19), kind=kLoop, calls=%fused_computation.11 | loop fusion | bytes 260 | tf_op jit(solution)/shard_map/dynamic_slice | solution.py:362
  56.9 3.9 %convolution_convert_fusion = bf16[288,4096]{1,0:T(8,128)(2,1)} fusion(bf16[256,4096]{1,0:T(8,128)(2,1)} %bitcast.8, bf16[320,256]{1,0:T(8,128)(2,1)} %get-tuple-element.5), kind=kOutput, calls=%fused_computation | convolution fusion | flops 605159424 | bytes 4603904 | tf_op jit(solution)/shard_map/ti,ip->tp/dot_general | solution.py:360
  (4 shorter events, 0.0 us)

commit v2 on v1

--- a/solution.py
+++ b/solution.py
@@ -78,7 +78,7 @@
     return (template_means, image_duals)
 
 
-def gather_and_plan(dims, img_hbm, tpl_hbm, info_ref, tlog_ref, gath_hbm, plan_ref, dual_ref,
+def gather_and_plan(dims, img_hbm, tpl_hbm, routes_ref, iw_ref, tw_ref, gath_hbm, plan_ref, dual_ref,
                     buf, infos, tpl, acc, parts, lse_out, lse_in,
                     send_sem, recv_sem, info_send, info_recv, local_sem,
                     part_send, part_recv, lse_send, lse_recv, plan_send, plan_recv):
@@ -94,11 +94,15 @@
     allowed = {UP: has_up, DOWN: has_down}
 
     tpl_copy = pltpu.make_async_copy(tpl_hbm, tpl, local_sem.at[0])
-    own_copy = pltpu.make_async_copy(img_hbm, buf.at[b], local_sem.at[1])
-    info_copy = pltpu.make_async_copy(info_ref, infos.at[b], local_sem.at[2])
     tpl_copy.start()
-    own_copy.start()
-    info_copy.start()
+
+    names = routes_ref[...].astype(jnp.float32) + 1.0
+    logs = jnp.log(iw_ref[...])
+    infos[b] = jnp.zeros(infos.shape[1:], jnp.float32)
+    for k in range(blocks):
+        window = slice(k * rows, (k + 1) * rows)
+        infos[b, 0:admits, window] = jnp.where(b == k, names, 0.0)
+        infos[b, admits:admits + 1, window] = jnp.where(b == k, logs, 0.0)
 
     barrier = pltpu.get_barrier_semaphore()
     for way in (UP, DOWN):
@@ -116,19 +120,19 @@
 
     def piece(way, k, c, own=False):
         return pltpu.make_async_remote_copy(
-            src_ref=img_hbm.at[:, cols(c)] if own else buf.at[k, :, cols(c)],
-            dst_ref=buf.at[k, :, cols(c)],
+            src_ref=img_hbm.at[:, cols(c)] if own else buf.at[c, k],
+            dst_ref=buf.at[c, k],
             send_sem=send_sem.at[way, k], recv_sem=recv_sem.at[k, c],
             device_id={"blk": target[way]}, device_id_type=MESH)
 
-    def info_piece(way, k, own=False):
+    def info_piece(way, k):
         return pltpu.make_async_remote_copy(
-            src_ref=info_ref if own else infos.at[k], dst_ref=infos.at[k],
+            src_ref=infos.at[k], dst_ref=infos.at[k],
             send_sem=info_send.at[way, k], recv_sem=info_recv.at[k],
             device_id={"blk": target[way]}, device_id_type=MESH)
 
     def arrived(k, c):
-        pltpu.make_async_copy(buf.at[k, :, cols(c)], buf.at[k, :, cols(c)], recv_sem.at[k, c]).wait()
+        pltpu.make_async_copy(buf.at[c, k], buf.at[c, k], recv_sem.at[k, c]).wait()
 
     def info_arrived(k):
         pltpu.make_async_copy(infos.at[k], infos.at[k], info_recv.at[k]).wait()
@@ -142,9 +146,11 @@
         piece(ACROSS, b, c, True).start()
         for way in (UP, DOWN):
             along(way, lambda: piece(way, b, c, True).start())
-    info_piece(ACROSS, b, True).start()
+    for c in range(CHUNKS):
+        pltpu.make_async_copy(img_hbm.at[:, cols(c)], buf.at[c, b], local_sem.at[1]).start()
+    info_piece(ACROSS, b).start()
     for way in (UP, DOWN):
-        along(way, lambda: info_piece(way, b, True).start())
+        along(way, lambda: info_piece(way, b).start())
     mate = z * LINES + other
     arrived(mate, 0)
     for way in (UP, DOWN):
@@ -186,7 +192,7 @@
                         arrived(from_z * LINES + other, c)
 
     def product(c):
-        images = buf[:, :, c * width:(c + 1) * width].reshape(blocks * rows, width)
+        images = buf[c].reshape(blocks * rows, width)
         term = lax.dot_general(tpl[:, c * width:(c + 1) * width], images, (((1,), (1,)), ((), ())),
                                preferred_element_type=jnp.float32)
         if c == 1:
@@ -198,7 +204,7 @@
         for c in range(CHUNKS):
             pass_on(d, c)
         pass_rest(d)
-    own_copy.wait()
+    pltpu.make_async_copy(buf.at[:, b], buf.at[:, b], local_sem.at[1]).wait()
     tpl_copy.wait()
     if share * pixes > tpl_dev:
         acc[tpl_dev:, :] = jnp.zeros((share * pixes - tpl_dev, blocks * rows), jnp.float32)
@@ -224,7 +230,6 @@
     back = pltpu.make_async_copy(buf, gath_hbm, local_sem.at[3])
     back.start()
 
-    info_copy.wait()
     info_arrived(mate)
     for d in range(1, depth):
         for way, from_z, there in sides(d):
@@ -236,7 +241,9 @@
     admitted = jnp.max(jnp.where(info[0:admits, :] == code, 1.0, 0.0), axis=0, keepdims=True)
     image_log = info[admits:admits + 1, :]
     first = p * share
-    template_log = tlog_ref[pl.ds(pl.multiple_of(first, 16), share), :]
+    here = (lax.broadcasted_iota(jnp.int32, (share, tpl_dev), 0) + first
+            == lax.broadcasted_iota(jnp.int32, (share, tpl_dev), 1))
+    template_log = jnp.sum(jnp.where(here, jnp.log(tw_ref[...]), 0.0), axis=1, keepdims=True)
     valid = first + lax.broadcasted_iota(jnp.int32, (share, 1), 0) < tpl_dev
     scores = acc[pl.ds(pl.multiple_of(first, 16), share), :]
     for j in range(1, pixes):
@@ -272,7 +279,10 @@
         every = lse_in[sweep]
         peak = jnp.max(every, axis=0)
         duals = image_log - peak - jnp.log(jnp.sum(jnp.exp(every - peak), axis=0))
-    dual_ref[...] = duals
+    mine_only = jnp.zeros((1, rows), jnp.float32)
+    for k in range(blocks):
+        mine_only = jnp.where(b == k, duals[:, k * rows:(k + 1) * rows], mine_only)
+    dual_ref[...] = mine_only
     terms = scores + duals
     weight = jnp.exp(terms - jnp.max(terms, axis=1, keepdims=True))
     mine = pl.ds(pl.multiple_of(first, 16), share)
@@ -287,9 +297,9 @@
     for j in range(1, pixes):
         my_plan(j).start()
 
-    full = buf.at[b]
-    rest = buf.at[b, :, pl.ds(width, pixels - width)]
-    one = buf.at[b, :, pl.ds(0, width)]
+    full = buf.at[:, b]
+    rest = buf.at[pl.ds(1, CHUNKS - 1), b]
+    one = buf.at[0, b]
 
     def left(ref, sem):
         pltpu.make_async_copy(ref, ref, sem).wait()
@@ -320,31 +330,33 @@
         my_plan(j).wait_recv()
 
 
+def average(plan_ref, img_ref, out_ref):
+    _, blocks, rows, width = img_ref.shape
+    images = img_ref[0].reshape(blocks * rows, width)
+    out_ref[...] = jnp.dot(plan_ref[0:out_ref.shape[0], :], images,
+                           preferred_element_type=jnp.float32).astype(out_ref.dtype)
+
+
 def gathered(images, templates, routes, image_weight, template_weight):
     blocks, pixes = lax.axis_size("blk"), lax.axis_size("pix")
     rows, pixels = images.shape
     tpl_dev, admits = templates.shape[0], routes.shape[1]
     share = -(-tpl_dev // (16 * pixes)) * 16
-    b = lax.axis_index("blk")
-    info = jnp.concatenate([routes.T.astype(jnp.float32) + 1.0, jnp.log(image_weight)[None, :]], axis=0)
-    info = jnp.pad(info, ((0, -(admits + 1) % 8), (0, 0)))
-    deep = info.shape[0]
-    spot = jnp.arange(blocks * rows, dtype=jnp.int32)[None, :] // rows == b
-    info = jnp.where(spot, jnp.tile(info, (1, blocks)), 0.0)
-    tlog = jnp.pad(jnp.log(template_weight), (0, share * pixes - tpl_dev))[:, None]
+    deep = -(-(admits + 1) // 8) * 8
+    width = pixels // CHUNKS
     dims = (blocks, pixes, admits, tpl_dev, share)
     any_spec, vmem = pl.BlockSpec(memory_space=pl.ANY), pl.BlockSpec(memory_space=pltpu.VMEM)
     dma = pltpu.SemaphoreType.DMA
     devices = blocks * pixes
     gath, plan, duals = pl.pallas_call(
         functools.partial(gather_and_plan, dims),
-        out_shape=(jax.ShapeDtypeStruct((blocks, rows, pixels), images.dtype),
+        out_shape=(jax.ShapeDtypeStruct((CHUNKS, blocks, rows, width), images.dtype),
                    jax.ShapeDtypeStruct((share * pixes, blocks * rows), jnp.bfloat16),
-                   jax.ShapeDtypeStruct((1, blocks * rows), jnp.float32)),
-        in_specs=[any_spec, any_spec, vmem, vmem],
+                   jax.ShapeDtypeStruct((1, rows), jnp.float32)),
+        in_specs=[any_spec, any_spec, vmem, vmem, vmem],
         out_specs=(any_spec, vmem, vmem),
         scratch_shapes=[
-            pltpu.VMEM((blocks, rows, pixels), images.dtype),
+            pltpu.VMEM((CHUNKS, blocks, rows, width), images.dtype),
             pltpu.VMEM((blocks, deep, blocks * rows), jnp.float32),
             pltpu.VMEM((tpl_dev, pixels), templates.dtype),
             pltpu.VMEM((share * pixes, blocks * rows), jnp.float32),
@@ -356,10 +368,16 @@
             dma((pixes - 1,)), dma((pixes - 1,)),
         ],
         compiler_params=pltpu.CompilerParams(collective_id=0, has_side_effects=True),
-    )(images, templates, info, tlog)
-    means = jnp.einsum("ti,ip->tp", plan[:tpl_dev], gath.reshape(blocks * rows, pixels),
-                       preferred_element_type=jnp.float32).astype(jnp.bfloat16)
-    return means, lax.dynamic_slice(duals.reshape(-1), (b * rows,), (rows,))
+    )(images, templates, routes.T, image_weight[None, :], template_weight[None, :])
+    means = pl.pallas_call(
+        average,
+        grid=(CHUNKS,),
+        out_shape=jax.ShapeDtypeStruct((tpl_dev, pixels), jnp.bfloat16),
+        in_specs=[pl.BlockSpec((share * pixes, blocks * rows), lambda c: (0, 0)),
+                  pl.BlockSpec((1, blocks, rows, width), lambda c: (c, 0, 0, 0))],
+        out_specs=pl.BlockSpec((tpl_dev, width), lambda c: (0, c)),
+    )(plan, gath)
+    return means, duals.reshape(-1)
 
 
 def on_device(images, templates, routes, image_weight, template_weight):

time: 61 us -> 60.6 us (level)
  Pallas kernels: 51.4 us -> 57.9 us
  matrix products: 3.87 us -> 0 us
  local copies, waits for them, and re-layouts: 3.46 us -> 1.76 us
  other arithmetic: 1.32 us -> 0 us
    pallas_call x0 -> x1, Pallas kernels: none -> 6.54 us  [gathered(): pl.pallas_call(average, grid=(CHUNKS,), out_shape=jax.ShapeDtypeStruct((t...]
    dot_general x1 -> x0, matrix products: 3.87 us -> none  [gathered(): jnp.einsum('ti,ip->tp', plan[:tpl_dev], gath.reshape(blocks * rows, pixel...]
    dynamic_slice x1 -> x0, local copies, waits for them, and re-layouts: 1.25 us -> none  [gathered(): return (means, lax.dynamic_slice(duals.reshape(-1), (b * rows,), (rows,)))]
    add x1 -> x0, other arithmetic: 0.69 us -> none  [gathered(): routes.T.astype(jnp.float32) + 1.0]
    log x1 -> x0, local copies, waits for them, and re-layouts: 0.68 us -> none  [gathered(): jnp.log(template_weight)]
    broadcast_in_dim x2 -> x1, local copies, waits for them, and re-layouts: 1.43 us -> 1.25 us  [gathered(): template_weight[None, :]]
where the time goes in v2:
time: 60.6 us; the launch traced here: 60.3 us
  Pallas kernels  57.9 us (96%)
  local copies, waits for them, and re-layouts  1.76 us (3%)
  between operations  0.65 us (1%)
    pallas_call x1, Pallas kernels, gathered(): pl.pallas_call(functools.partial(gather_and_plan, dims), out_shape=(jax.S...  51.3 us
    pallas_call x1, Pallas kernels, gathered(): pl.pallas_call(average, grid=(CHUNKS,), out_shape=jax.ShapeDtypeStruct((t...  6.54 us
    broadcast_in_dim x1, local copies, waits for them, and re-layouts, gathered(): template_weight[None, :]  1.25 us

profile of v2, /device:TPU:0, one launch (start us, length us, event | category | flops | bytes accessed | tf_op | source)
XLA Modules:
  0.0 60.3 jit_solution(2580804673065229501)
XLA Ops:
  0.6 1.2 %broadcast_in_dim.7.tw_ref = f32[1,288]{1,0:T(1,128)} reshape(f32[288]{0:T(512)} %param.9) | data formatting | bytes 2304 | tf_op jit(solution)/shard_map/broadcast_in_dim | solution.py:371
  1.9 51.3 %shard_map.68 = (bf16[8,8,32,512]{3,2,1,0:T(8,128)(2,1)}, bf16[320,256]{1,0:T(8,128)(2,1)}, f32[1,32]{1,0:T(1,128)}) custom-call(bf16[32,4096]{1,0:T(8,128)(2,1)} %img_hbm.1, bf16[288,4096]{1,0:T(8,128)(2,1)} %tpl_hbm.1, s32[4,32]{1,0:T(4,128)} %bitcast.3, f32[1,32]{1,0:T(1,128)} %bitcast.4, f32[1,288]{1,0:T(1,128)} %broadcast_in_dim.7.tw_ref), custom_call_target="tpu_custom_call" | custom-call | tf_op jit(solution)/shard_map/pallas_call | solution.py:351
  53.2 0.0 copy-start
  53.2 6.5 %shard_map.69 = bf16[288,4096]{1,0:T(8,128)(2,1)} custom-call(bf16[320,256]{1,0:T(8,128)(2,1)} %get-tuple-element.5.plan_ref, bf16[8,8,32,512]{3,2,1,0:T(8,128)(2,1)} %get-tuple-element.6.img_ref), custom_call_target="tpu_custom_call" | custom-call | tf_op jit(solution)/shard_map/pallas_call | solution.py:372
  59.8 0.0 copy-done
  59.8 0.5 copy.8
Async XLA Ops:
  53.2 6.6 %copy-start = (f32[1,32]{1,0:T(1,128)S(1)}, f32[1,32]{1,0:T(1,128)}, u32[]{:S(2)}) copy-start(f32[1,32]{1,0:T(1,128)} %get-tuple-element.7) | copy-start | bytes 388

commit v3 on v2

--- a/solution.py
+++ b/solution.py
@@ -227,8 +227,8 @@
 
     for j in range(1, pixes):
         my_part(j).start()
-    back = pltpu.make_async_copy(buf, gath_hbm, local_sem.at[3])
-    back.start()
+    for c in range(CHUNKS):
+        pltpu.make_async_copy(buf.at[c], gath_hbm.at[:, :, cols(c)], local_sem.at[3]).start()
 
     info_arrived(mate)
     for d in range(1, depth):
@@ -243,7 +243,7 @@
     first = p * share
     here = (lax.broadcasted_iota(jnp.int32, (share, tpl_dev), 0) + first
             == lax.broadcasted_iota(jnp.int32, (share, tpl_dev), 1))
-    template_log = jnp.sum(jnp.where(here, jnp.log(tw_ref[...]), 0.0), axis=1, keepdims=True)
+    template_log = jnp.sum(jnp.where(here, jnp.log(tw_ref[...].reshape(1, tpl_dev)), 0.0), axis=1, keepdims=True)
     valid = first + lax.broadcasted_iota(jnp.int32, (share, 1), 0) < tpl_dev
     scores = acc[pl.ds(pl.multiple_of(first, 16), share), :]
     for j in range(1, pixes):
@@ -324,17 +324,10 @@
     for sweep in range(SWEEPS):
         span = lse_in.at[sweep, pl.ds(0, devices - 1)]
         left(span, lse_send.at[sweep])
-    back.wait()
+    left(buf, local_sem.at[3])
     for j in range(1, pixes):
         my_plan(j).wait_send()
         my_plan(j).wait_recv()
-
-
-def average(plan_ref, img_ref, out_ref):
-    _, blocks, rows, width = img_ref.shape
-    images = img_ref[0].reshape(blocks * rows, width)
-    out_ref[...] = jnp.dot(plan_ref[0:out_ref.shape[0], :], images,
-                           preferred_element_type=jnp.float32).astype(out_ref.dtype)
 
 
 def gathered(images, templates, routes, image_weight, template_weight):
@@ -350,7 +343,7 @@
     devices = blocks * pixes
     gath, plan, duals = pl.pallas_call(
         functools.partial(gather_and_plan, dims),
-        out_shape=(jax.ShapeDtypeStruct((CHUNKS, blocks, rows, width), images.dtype),
+        out_shape=(jax.ShapeDtypeStruct((blocks, rows, pixels), images.dtype),
                    jax.ShapeDtypeStruct((share * pixes, blocks * rows), jnp.bfloat16),
                    jax.ShapeDtypeStruct((1, rows), jnp.float32)),
         in_specs=[any_spec, any_spec, vmem, vmem, vmem],
@@ -368,15 +361,9 @@
             dma((pixes - 1,)), dma((pixes - 1,)),
         ],
         compiler_params=pltpu.CompilerParams(collective_id=0, has_side_effects=True),
-    )(images, templates, routes.T, image_weight[None, :], template_weight[None, :])
-    means = pl.pallas_call(
-        average,
-        grid=(CHUNKS,),
-        out_shape=jax.ShapeDtypeStruct((tpl_dev, pixels), jnp.bfloat16),
-        in_specs=[pl.BlockSpec((share * pixes, blocks * rows), lambda c: (0, 0)),
-                  pl.BlockSpec((1, blocks, rows, width), lambda c: (c, 0, 0, 0))],
-        out_specs=pl.BlockSpec((tpl_dev, width), lambda c: (0, c)),
-    )(plan, gath)
+    )(images, templates, routes.T, image_weight[None, :], template_weight)
+    means = jnp.einsum("ti,ip->tp", plan[:tpl_dev], gath.reshape(blocks * rows, pixels),
+                       preferred_element_type=jnp.float32).astype(jnp.bfloat16)
     return means, duals.reshape(-1)
 
 

time: 60.6 us -> 56.5 us (0.932)
  Pallas kernels: 57.9 us -> 51.3 us
  matrix products: 0 us -> 3.87 us
  local copies, waits for them, and re-layouts: 1.76 us -> 0.52 us
    pallas_call x1 -> x0, Pallas kernels: 6.54 us -> none  [gathered(): pl.pallas_call(average, grid=(CHUNKS,), out_shape=jax.ShapeDtypeStruct((t...]
    dot_general x0 -> x1, matrix products: none -> 3.87 us  [gathered(): jnp.einsum('ti,ip->tp', plan[:tpl_dev], gath.reshape(blocks * rows, pixel...]
    broadcast_in_dim x1 -> x0, local copies, waits for them, and re-layouts: 1.25 us -> none  [gathered(): template_weight[None, :]]
where the time goes in v3:
time: 56.5 us; the launch traced here: 56.4 us
  Pallas kernels  51.3 us (91%)
  matrix products  3.87 us (7%)
  between operations  0.65 us (1%)
    pallas_call x1, Pallas kernels, gathered(): pl.pallas_call(functools.partial(gather_and_plan, dims), out_shape=(jax.S...  51.3 us
    dot_general x1, matrix products, gathered(): jnp.einsum('ti,ip->tp', plan[:tpl_dev], gath.reshape(blocks * rows, pixel...  3.87 us

profile of v3, /device:TPU:0, one launch (start us, length us, event | category | flops | bytes accessed | tf_op | source)
XLA Modules:
  0.0 56.4 jit_solution(3980003671887719903)
XLA Ops:
  0.6 51.3 %shard_map.68 = (bf16[8,32,4096]{2,1,0:T(8,128)(2,1)}, bf16[320,256]{1,0:T(8,128)(2,1)}, f32[1,32]{1,0:T(1,128)}) custom-call(bf16[32,4096]{1,0:T(8,128)(2,1)} %img_hbm.1, bf16[288,4096]{1,0:T(8,128)(2,1)} %tpl_hbm.1, s32[4,32]{1,0:T(4,128)} %bitcast.6, f32[1,32]{1,0:T(1,128)} %bitcast.7, f32[288]{0:T(512)} %tw_ref.1), custom_call_target="tpu_custom_call" | custom-call | tf_op jit(solution)/shard_map/pallas_call | solution.py:344
  52.0 0.0 copy-start
  52.0 3.9 %convolution_convert_fusion = bf16[288,4096]{1,0:T(8,128)(2,1)} fusion(bf16[256,4096]{1,0:T(8,128)(2,1)} %bitcast.5, bf16[320,256]{1,0:T(8,128)(2,1)} %get-tuple-element.5), kind=kOutput, calls=%fused_computation | convolution fusion | flops 605159424 | bytes 4603904 | tf_op jit(solution)/shard_map/ti,ip->tp/dot_general | solution.py:365
  55.8 0.0 copy-done
  55.8 0.5 copy.8
Async XLA Ops:
  52.0 3.9 %copy-start = (f32[1,32]{1,0:T(1,128)S(1)}, f32[1,32]{1,0:T(1,128)}, u32[]{:S(2)}) copy-start(f32[1,32]{1,0:T(1,128)} %get-tuple-element.7) | copy-start | bytes 388

commit v4 on v3

--- a/solution.py
+++ b/solution.py
@@ -182,23 +182,37 @@
                 info_piece(ACROSS, k).start()
                 along(way, lambda: info_piece(way, k).start())
 
-    def crossed(c):
+    half_z = depth // 2
+    half = blocks // 2
+    h = z // half_z
+
+    def crossed(c, early):
         if c:
-            arrived(mate, c)
-            for d in range(1, depth):
+            if early:
+                arrived(mate, c)
+            for d in range(1, half_z if early else depth):
                 for way, from_z, there in sides(d):
-                    @pl.when(there)
+                    same = (from_z >= h * half_z) & (from_z < (h + 1) * half_z)
+
+                    @pl.when(there & (same if early else jnp.logical_not(same)))
                     def _():
                         arrived(from_z * LINES + other, c)
 
-    def product(c):
-        images = buf[c].reshape(blocks * rows, width)
+    def product(c, side, fresh):
+        images = buf[c, pl.ds(side * half, half)].reshape(half * rows, width)
         term = lax.dot_general(tpl[:, c * width:(c + 1) * width], images, (((1,), (1,)), ((), ())),
                                preferred_element_type=jnp.float32)
-        if c == 1:
-            acc[0:tpl_dev, :] = term
+        if fresh:
+            acc[side, 0:tpl_dev, :] = term
         else:
-            acc[0:tpl_dev, :] += term
+            acc[side, 0:tpl_dev, :] += term
+
+    def my_part(e, j):
+        return pltpu.make_async_remote_copy(
+            src_ref=acc.at[h if e == 0 else 1 - h, pl.ds(lax.rem(p + j, pixes) * share, share), :],
+            dst_ref=parts.at[e, j - 1],
+            send_sem=part_send.at[e, j - 1], recv_sem=part_recv.at[e, j - 1],
+            device_id={"pix": lax.rem(p + j, pixes)}, device_id_type=MESH)
 
     for d in range(1, depth - 1):
         for c in range(CHUNKS):
@@ -207,26 +221,25 @@
     pltpu.make_async_copy(buf.at[:, b], buf.at[:, b], local_sem.at[1]).wait()
     tpl_copy.wait()
     if share * pixes > tpl_dev:
-        acc[tpl_dev:, :] = jnp.zeros((share * pixes - tpl_dev, blocks * rows), jnp.float32)
+        acc[:, tpl_dev:, :] = jnp.zeros((2, share * pixes - tpl_dev, half * rows), jnp.float32)
+    for c in range(CHUNKS):
+        crossed(c, True)
+        product(c, h, c == 0)
+    for j in range(1, pixes):
+        my_part(0, j).start()
     for c in range(CHUNKS + LAG):
         if c < CHUNKS:
             pass_on(depth - 1, c)
         if c == CHUNKS - 1:
             pass_rest(depth - 1)
         if c == CHUNKS + LAG - 1:
-            product(0)
+            product(0, 1 - h, False)
         if c > LAG:
-            crossed(c - LAG)
-            product(c - LAG)
-
-    def my_part(j):
-        return pltpu.make_async_remote_copy(
-            src_ref=acc.at[pl.ds(lax.rem(p + j, pixes) * share, share), :], dst_ref=parts.at[j - 1],
-            send_sem=part_send.at[j - 1], recv_sem=part_recv.at[j - 1],
-            device_id={"pix": lax.rem(p + j, pixes)}, device_id_type=MESH)
-
-    for j in range(1, pixes):
-        my_part(j).start()
+            crossed(c - LAG, False)
+            product(c - LAG, 1 - h, c - LAG == 1)
+
+    for j in range(1, pixes):
+        my_part(1, j).start()
     for c in range(CHUNKS):
         pltpu.make_async_copy(buf.at[c], gath_hbm.at[:, :, cols(c)], local_sem.at[3]).start()
 
@@ -245,10 +258,14 @@
             == lax.broadcasted_iota(jnp.int32, (share, tpl_dev), 1))
     template_log = jnp.sum(jnp.where(here, jnp.log(tw_ref[...].reshape(1, tpl_dev)), 0.0), axis=1, keepdims=True)
     valid = first + lax.broadcasted_iota(jnp.int32, (share, 1), 0) < tpl_dev
-    scores = acc[pl.ds(pl.multiple_of(first, 16), share), :]
-    for j in range(1, pixes):
-        my_part(j).wait_recv()
-        scores = scores + parts[j - 1]
+    sums = []
+    for e, side in ((0, h), (1, 1 - h)):
+        total = acc[side, pl.ds(pl.multiple_of(first, 16), share), :]
+        for j in range(1, pixes):
+            my_part(e, j).wait_recv()
+            total = total + parts[e, j - 1]
+        sums.append(total)
+    scores = jnp.concatenate([jnp.where(h == 0, sums[0], sums[1]), jnp.where(h == 0, sums[1], sums[0])], axis=1)
     scores = jnp.where(admitted > 0, scores, NEG)
 
     me = b * pixes + p
@@ -320,7 +337,8 @@
                 along(way, lambda: (left(full, send_sem.at[way, k]), left(one, send_sem.at[way, k2]),
                                     left(infos.at[b], info_send.at[way, k])) and None)
     for j in range(1, pixes):
-        my_part(j).wait_send()
+        my_part(0, j).wait_send()
+        my_part(1, j).wait_send()
     for sweep in range(SWEEPS):
         span = lse_in.at[sweep, pl.ds(0, devices - 1)]
         left(span, lse_send.at[sweep])
@@ -352,12 +370,12 @@
             pltpu.VMEM((CHUNKS, blocks, rows, width), images.dtype),
             pltpu.VMEM((blocks, deep, blocks * rows), jnp.float32),
             pltpu.VMEM((tpl_dev, pixels), templates.dtype),
-            pltpu.VMEM((share * pixes, blocks * rows), jnp.float32),
-            pltpu.VMEM((pixes - 1, share, blocks * rows), jnp.float32),
+            pltpu.VMEM((2, share * pixes, blocks * rows // 2), jnp.float32),
+            pltpu.VMEM((2, pixes - 1, share, blocks * rows // 2), jnp.float32),
             pltpu.VMEM((SWEEPS, 1, blocks * rows), jnp.float32),
             pltpu.VMEM((SWEEPS, devices, 1, blocks * rows), jnp.float32),
             dma((3, blocks)), dma((blocks, CHUNKS)), dma((3, blocks)), dma((blocks,)), dma((4,)),
-            dma((pixes - 1,)), dma((pixes - 1,)), dma((SWEEPS,)), dma((SWEEPS,)),
+            dma((2, pixes - 1)), dma((2, pixes - 1)), dma((SWEEPS,)), dma((SWEEPS,)),
             dma((pixes - 1,)), dma((pixes - 1,)),
         ],
         compiler_params=pltpu.CompilerParams(collective_id=0, has_side_effects=True),
@@ -369,7 +387,7 @@
 
 def on_device(images, templates, routes, image_weight, template_weight):
     blocks = lax.axis_size("blk")
-    if blocks * images.shape[0] <= templates.shape[0] and blocks % LINES == 0:
+    if blocks * images.shape[0] <= templates.shape[0] and blocks % (2 * LINES) == 0:
         return gathered(images, templates, routes, image_weight, template_weight)
     return routed(images, templates, routes, image_weight, template_weight)
 

time: 56.5 us -> 56.1 us (level)
  no operation moved by 1% of the time
where the time goes in v4:
time: 56.1 us; the launch traced here: 55.9 us
  Pallas kernels  50.9 us (91%)
  matrix products  3.87 us (7%)
  between operations  0.65 us (1%)
    pallas_call x1, Pallas kernels, gathered(): pl.pallas_call(functools.partial(gather_and_plan, dims), out_shape=(jax.S...  50.9 us
    dot_general x1, matrix products, gathered(): jnp.einsum('ti,ip->tp', plan[:tpl_dev], gath.reshape(blocks * rows, pixel...  3.87 us

profile of v4, /device:TPU:0, one launch (start us, length us, event | category | flops | bytes accessed | tf_op | source)
XLA Modules:
  0.0 55.9 jit_solution(15514865648976860854)
XLA Ops:
  0.6 50.9 %shard_map.68 = (bf16[8,32,4096]{2,1,0:T(8,128)(2,1)}, bf16[320,256]{1,0:T(8,128)(2,1)}, f32[1,32]{1,0:T(1,128)}) custom-call(bf16[32,4096]{1,0:T(8,128)(2,1)} %img_hbm.1, bf16[288,4096]{1,0:T(8,128)(2,1)} %tpl_hbm.1, s32[4,32]{1,0:T(4,128)} %bitcast.6, f32[1,32]{1,0:T(1,128)} %bitcast.7, f32[288]{0:T(512)} %tw_ref.1), custom_call_target="tpu_custom_call" | custom-call | tf_op jit(solution)/shard_map/pallas_call | solution.py:362
  51.5 0.0 copy-start
  51.5 3.9 %convolution_convert_fusion = bf16[288,4096]{1,0:T(8,128)(2,1)} fusion(bf16[256,4096]{1,0:T(8,128)(2,1)} %bitcast.5, bf16[320,256]{1,0:T(8,128)(2,1)} %get-tuple-element.5), kind=kOutput, calls=%fused_computation | convolution fusion | flops 605159424 | bytes 4603904 | tf_op jit(solution)/shard_map/ti,ip->tp/dot_general | solution.py:383
  55.4 0.0 copy-done
  55.4 0.5 copy.8
Async XLA Ops:
  51.5 3.9 %copy-start = (f32[1,32]{1,0:T(1,128)S(1)}, f32[1,32]{1,0:T(1,128)}, u32[]{:S(2)}) copy-start(f32[1,32]{1,0:T(1,128)} %get-tuple-element.7) | copy-start | bytes 388

commit v5 on v4

--- a/solution.py
+++ b/solution.py
@@ -8,7 +8,7 @@
 
 SWEEPS = 2
 LINES = 2
-CHUNKS = 8
+CHUNKS = 4
 LAG = 2
 NEG = -1e30
 MESH = pl.DeviceIdType.MESH

time: 56.1 us -> 55 us (0.980)
  Pallas kernels: 50.9 us -> 49.8 us
    pallas_call x1, Pallas kernels: 50.9 us -> 49.8 us  [gathered(): pl.pallas_call(functools.partial(gather_and_plan, dims), out_shape=(jax.S...]
where the time goes in v5:
time: 55 us; the launch traced here: 54.9 us
  Pallas kernels  49.8 us (91%)
  matrix products  3.87 us (7%)
  between operations  0.65 us (1%)
    pallas_call x1, Pallas kernels, gathered(): pl.pallas_call(functools.partial(gather_and_plan, dims), out_shape=(jax.S...  49.8 us
    dot_general x1, matrix products, gathered(): jnp.einsum('ti,ip->tp', plan[:tpl_dev], gath.reshape(blocks * rows, pixel...  3.87 us

profile of v5, /device:TPU:0, one launch (start us, length us, event | category | flops | bytes accessed | tf_op | source)
XLA Modules:
  0.0 54.9 jit_solution(4162865747187915487)
XLA Ops:
  0.6 49.8 %shard_map.68 = (bf16[8,32,4096]{2,1,0:T(8,128)(2,1)}, bf16[320,256]{1,0:T(8,128)(2,1)}, f32[1,32]{1,0:T(1,128)}) custom-call(bf16[32,4096]{1,0:T(8,128)(2,1)} %img_hbm.1, bf16[288,4096]{1,0:T(8,128)(2,1)} %tpl_hbm.1, s32[4,32]{1,0:T(4,128)} %bitcast.6, f32[1,32]{1,0:T(1,128)} %bitcast.7, f32[288]{0:T(512)} %tw_ref.1), custom_call_target="tpu_custom_call" | custom-call | tf_op jit(solution)/shard_map/pallas_call | solution.py:362
  50.5 0.0 copy-start
  50.5 3.9 %convolution_convert_fusion = bf16[288,4096]{1,0:T(8,128)(2,1)} fusion(bf16[256,4096]{1,0:T(8,128)(2,1)} %bitcast.5, bf16[320,256]{1,0:T(8,128)(2,1)} %get-tuple-element.5), kind=kOutput, calls=%fused_computation | convolution fusion | flops 605159424 | bytes 4603904 | tf_op jit(solution)/shard_map/ti,ip->tp/dot_general | solution.py:383
  54.3 0.0 copy-done
  54.3 0.5 copy.8
Async XLA Ops:
  50.5 3.9 %copy-start = (f32[1,32]{1,0:T(1,128)S(1)}, f32[1,32]{1,0:T(1,128)}, u32[]{:S(2)}) copy-start(f32[1,32]{1,0:T(1,128)} %get-tuple-element.7) | copy-start | bytes 388
